TPU v7x, 256 devices: a whole 4x4x8 slice. The times are simulated.
256 devices in a mesh: rows: 32 (over y, z), tensor: 8 (over x, core).
Axes of the slice: x: 4, y: 4, z: 8, core: 2. Of those that a mesh axis runs over, the one named last changes fastest.
Arguments:
- token_ids: int32 [256, 4], replicated, may hold values from 0 to 65535
- cache_lengths: int32 [256], P('rows'), may hold values from 160 to 1280, as said below
- doc_ids: int32 [256], replicated, may hold values from 0 to 31
- embed_table: bfloat16 [65536, 8192], P('tensor', 'rows'), may hold values from -10.5 to 10.5
- cache_keys: bfloat16 [256, 1280, 1024], P('rows', None, 'tensor'), may hold values from -700 to 700
- cache_values: bfloat16 [256, 1280, 1024], P('rows', None, 'tensor'), may hold values from -6 to 6
- decode_gain: float32 [8192], P('rows'), may hold values from 0.1 to 1.9
- decode_query: bfloat16 [8192, 8192], P('rows', 'tensor'), may hold values from -0.0625 to 0.0625
- decode_key: bfloat16 [8192, 1024], P('rows', 'tensor'), may hold values from -0.0625 to 0.0625
- decode_value: bfloat16 [8192, 1024], P('rows', 'tensor'), may hold values from -0.0625 to 0.0625
- decode_out: bfloat16 [8192, 8192], P('tensor', 'rows'), may hold values from -0.0625 to 0.0625
- reduce_gain: float32 [8192], P('rows'), may hold values from 0.8 to 10
- reduce_query: bfloat16 [8192, 8192], P('rows', 'tensor'), may hold values from -0.0625 to 0.0625
- reduce_key: bfloat16 [8192, 1024], P('rows', 'tensor'), may hold values from -0.0625 to 0.0625
- reduce_value: bfloat16 [8192, 1024], P('rows', 'tensor'), may hold values from -0.0625 to 0.0625
- reduce_out: bfloat16 [8192, 8192], P('tensor', 'rows'), may hold values from -0.0625 to 0.0625
Outputs:
- reduced: bfloat16 [1024, 8192], P(None, 'rows')
Inputs may be any that keep to these rules, and one draw needn't show every extreme that they name: Passage row c holds cache entries at positions below cache_lengths[c]; one row in every draw has a full cache of 1280.
All inputs are finite; a program needn't handle non-finite values.
Results may differ from a plain program's by a relative error of at most 0.035.
The roundings to bfloat16 on the way count: a program that leaves them out, or rounds other values in their place, can miss the bound.
Values may be sent and summed in bfloat16 or wider, within the bound.
A program may use at most 64 MiB of HBM per device.

v0:
```python
import jax
import jax.numpy as jnp
from jax import lax
from jax.sharding import PartitionSpec as P

D = 8192
HEAD_DIM = 128
EPSILON = 1e-05
ROPE_BASE = 500000.0


def rotate(vectors, positions):
    half_dim = vectors.shape[-1] // 2
    frequencies = ROPE_BASE ** (-2.0 * jnp.arange(half_dim, dtype=jnp.float32) / vectors.shape[-1])
    angles = positions.astype(jnp.float32)[..., None] * frequencies
    cosine = jnp.cos(angles)
    sine_part = jnp.sin(angles)
    lower_half = vectors[..., :half_dim]
    upper_half = vectors[..., half_dim:]
    return jnp.concatenate(
        [
            lower_half * cosine - upper_half * sine_part,
            upper_half * cosine + lower_half * sine_part,
        ],
        axis=-1,
    )


def width_total(partial_value):
    return lax.psum(partial_value, "tensor")


def row_scale(summed):
    return lax.rsqrt(summed / D + EPSILON)


def head_terms(normed, matrices, squares, groups):
    partial = jnp.concatenate(
        [jnp.dot(normed, matrix, preferred_element_type=jnp.float32) for matrix in matrices], axis=1
    )
    tokens, cols = partial.shape
    own = tokens // groups
    payload = jnp.concatenate(
        [partial.reshape(groups, own * cols), squares.reshape(groups, own)], axis=1
    ).reshape(groups, 8, (own * cols + own) // 8)
    summed = lax.psum_scatter(payload, "rows", scatter_dimension=0, tiled=True)
    summed = summed.reshape(own * cols + own)
    return (summed[: own * cols].reshape(own, cols), summed[own * cols :])


def head_mix(attended, matrix):
    return jnp.dot(
        lax.all_gather(attended, "rows", axis=0, tiled=True),
        matrix,
        preferred_element_type=jnp.float32,
    )


def per_device(
    token_ids,
    cache_lengths,
    doc_ids,
    embed_table,
    cache_keys,
    cache_values,
    decode_gain,
    decode_query,
    decode_key,
    decode_value,
    decode_out,
    reduce_gain,
    reduce_query,
    reduce_key,
    reduce_value,
    reduce_out,
):
    step_count = token_ids.shape[1]
    passage_count = token_ids.shape[0]
    token_count = passage_count * step_count
    own_passages = cache_lengths.shape[0]
    own_tokens = own_passages * step_count
    row_first = lax.axis_index("rows") * own_tokens
    query_cols = decode_query.shape[1]
    kv_cols = decode_key.shape[1]
    local_heads = query_cols // HEAD_DIM
    local_kv = kv_cols // HEAD_DIM
    group_size = local_heads // local_kv
    score_scale = HEAD_DIM ** (-0.5)
    step_ids = jnp.arange(step_count, dtype=jnp.int32)
    vocab_part = embed_table.shape[0]
    local_ids = token_ids.reshape(token_count) - lax.axis_index("tensor") * vocab_part
    inside = (local_ids >= 0) & (local_ids < vocab_part)
    picked = jnp.take(embed_table, jnp.clip(local_ids, 0, vocab_part - 1), axis=0)
    picked = jnp.where(inside[:, None], picked, jnp.zeros_like(picked))
    embedded = width_total(picked).astype(jnp.float32)
    row_groups = token_count // own_tokens
    normed = (embedded * decode_gain[None, :]).astype(jnp.bfloat16)
    projected, dec_squares = head_terms(
        normed,
        (decode_query, decode_key, decode_value),
        jnp.sum(embedded * embedded, axis=1),
        row_groups,
    )
    projected = projected * row_scale(dec_squares)[:, None]
    positions = (cache_lengths[:, None] + step_ids[None, :]).reshape(own_tokens, 1)
    queries = rotate(
        projected[:, :query_cols].reshape(own_tokens, local_heads, HEAD_DIM), positions
    ).astype(jnp.bfloat16)
    keys_new = rotate(
        projected[:, query_cols : query_cols + kv_cols].reshape(own_tokens, local_kv, HEAD_DIM),
        positions,
    ).astype(jnp.bfloat16)
    values_new = projected[:, query_cols + kv_cols :].astype(jnp.bfloat16)
    queries = queries.reshape(own_passages, step_count, local_kv, group_size, HEAD_DIM)
    keys_new = keys_new.reshape(own_passages, step_count, local_kv, HEAD_DIM)
    values_new = values_new.reshape(own_passages, step_count, local_kv, HEAD_DIM)
    capacity = cache_keys.shape[1]
    keys_old = cache_keys.reshape(own_passages, capacity, local_kv, HEAD_DIM)
    values_old = cache_values.reshape(own_passages, capacity, local_kv, HEAD_DIM)
    new_scores = (
        jnp.einsum("rskgd,rtkd->rskgt", queries, keys_new, preferred_element_type=jnp.float32)
        * score_scale
    )
    causal = step_ids[None, :] <= step_ids[:, None]
    new_scores = jnp.where(causal[None, :, None, None, :], new_scores, -jnp.inf)
    old_scores = (
        jnp.einsum("rskgd,rckd->rskgc", queries, keys_old, preferred_element_type=jnp.float32)
        * score_scale
    )
    slot_ids = jnp.arange(capacity, dtype=jnp.int32)
    live_mask = slot_ids[None, :] < cache_lengths[:, None]
    old_scores = jnp.where(live_mask[:, None, None, None, :], old_scores, -jnp.inf)
    highest = jnp.maximum(jnp.max(old_scores, axis=-1), jnp.max(new_scores, axis=-1))
    old_exp = jnp.exp(old_scores - highest[..., None])
    new_exp = jnp.exp(new_scores - highest[..., None])
    summed = jnp.sum(old_exp, axis=-1) + jnp.sum(new_exp, axis=-1)
    old_weights = (old_exp / summed[..., None]).astype(jnp.bfloat16)
    new_weights = (new_exp / summed[..., None]).astype(jnp.bfloat16)
    attended = jnp.einsum(
        "rskgc,rckd->rskgd", old_weights, values_old, preferred_element_type=jnp.float32
    )
    attended = attended + jnp.einsum(
        "rskgt,rtkd->rskgd", new_weights, values_new, preferred_element_type=jnp.float32
    )
    attended = attended.reshape(own_tokens, query_cols).astype(jnp.bfloat16)
    partial_value = head_mix(attended, decode_out)
    summary = (embedded + width_total(partial_value)).astype(jnp.bfloat16)
    summary_wide = summary.astype(jnp.float32)
    normed_red = (summary_wide * reduce_gain[None, :]).astype(jnp.bfloat16)
    passage_index = jnp.arange(passage_count, dtype=jnp.int32)
    earlier = jnp.sum(
        (
            (doc_ids[None, :] == doc_ids[:, None])
            & (passage_index[None, :] < passage_index[:, None])
        ).astype(jnp.int32),
        axis=1,
    )
    doc_positions = (earlier[:, None] * step_count + step_ids[None, :]).reshape(token_count, 1)
    doc_tokens = (doc_ids[:, None] + jnp.zeros_like(step_ids)[None, :]).reshape(token_count)
    own_positions = lax.dynamic_slice_in_dim(doc_positions, row_first, own_tokens, 0)
    projected, red_squares = head_terms(
        normed_red,
        (reduce_query, reduce_key, reduce_value),
        jnp.sum(summary_wide * summary_wide, axis=1),
        row_groups,
    )
    projected = projected * row_scale(red_squares)[:, None]
    queries_red = rotate(
        projected[:, :query_cols].reshape(own_tokens, local_heads, HEAD_DIM), own_positions
    ).astype(jnp.bfloat16)
    keys_own = (
        rotate(
            projected[:, query_cols : query_cols + kv_cols].reshape(own_tokens, local_kv, HEAD_DIM),
            own_positions,
        )
        .astype(jnp.bfloat16)
        .reshape(own_tokens, kv_cols)
    )
    values_own = projected[:, query_cols + kv_cols :].astype(jnp.bfloat16)
    kv_red = lax.all_gather(
        jnp.concatenate([keys_own, values_own], axis=1), "rows", axis=0, tiled=True
    )
    keys_red, values_red = (kv_red[:, :kv_cols], kv_red[:, kv_cols:])
    queries_red = queries_red.reshape(own_tokens, local_kv, group_size, HEAD_DIM)
    keys_red = keys_red.reshape(token_count, local_kv, HEAD_DIM)
    values_red = values_red.reshape(token_count, local_kv, HEAD_DIM)
    token_index = jnp.arange(token_count, dtype=jnp.int32)
    own_index = row_first + jnp.arange(own_tokens, dtype=jnp.int32)
    own_docs = lax.dynamic_slice_in_dim(doc_tokens, row_first, own_tokens, 0)
    allowed = (own_docs[:, None] == doc_tokens[None, :]) & (
        token_index[None, :] <= own_index[:, None]
    )
    red_scores = (
        jnp.einsum("tkgd,ukd->tkgu", queries_red, keys_red, preferred_element_type=jnp.float32)
        * score_scale
    )
    red_scores = jnp.where(allowed[:, None, None, :], red_scores, -jnp.inf)
    red_high = jnp.max(red_scores, axis=-1)
    red_exp = jnp.exp(red_scores - red_high[..., None])
    red_weights = (red_exp / jnp.sum(red_exp, axis=-1)[..., None]).astype(jnp.bfloat16)
    red_out = jnp.einsum(
        "tkgu,ukd->tkgd", red_weights, values_red, preferred_element_type=jnp.float32
    )
    red_out = red_out.reshape(own_tokens, query_cols).astype(jnp.bfloat16)
    return (summary_wide + width_total(head_mix(red_out, reduce_out))).astype(jnp.bfloat16)


def solution(mesh):
    return jax.shard_map(
        per_device,
        mesh=mesh,
        in_specs=(
            P(),
            P("rows"),
            P(),
            P("tensor", "rows"),
            P("rows", None, "tensor"),
            P("rows", None, "tensor"),
            P("rows"),
            P("rows", "tensor"),
            P("rows", "tensor"),
            P("rows", "tensor"),
            P("tensor", "rows"),
            P("rows"),
            P("rows", "tensor"),
            P("rows", "tensor"),
            P("rows", "tensor"),
            P("tensor", "rows"),
        ),
        out_specs=P(None, "rows"),
        check_vma=False,
    )
```

profile of v0, /device:TPU:8, one launch (start us, length us, event | category | flops | bytes accessed | tf_op | source)
XLA Modules:
  0.0 927.0 jit_solution(14804765056638584329)
XLA Ops:
  6.5 0.9 subtract_clamp_fusion
  8.8 6.2 gather_fusion
  15.0 1.1 select_select_fusion
  16.3 69.0 %all-reduce.6.cloned.1.call-done = bf16[1024,256]{1,0:T(8,128)(2,1)} async-done(((bf16[1024,256]{1,0:T(8,128)(2,1)}), bf16[1024,256]{1,0:T(8,128)(2,1)}) %all-reduce.6.cloned.1.call-update) | async-done | bytes 524304 | tf_op jit(solution)/shard_map/psum | solution.py:30
  85.3 2.0 fusion.41
  88.0 2.8 pad_maximum_fusion.2
  90.8 5.9 copy.36
  96.7 5.6 reshape.597
  102.5 5.2 pad_maximum_fusion
  107.7 6.8 reshape.599
  116.9 209.4 %reduce-scatter.7.cloned.1.call-done = f32[1,8,5124]{2,1,0:T(8,128)} async-done(((f32[32,8,5124]{2,1,0:T(8,128)}), f32[1,8,5124]{2,1,0:T(8,128)}) %reduce-scatter.7.cloned.1.call-update) | async-done | bytes 163984
  326.3 1.0 reshape.600
  327.9 0.9 broadcast_multiply_fusion.1
  328.9 0.8 fusion.65
  329.9 1.1 fusion.81
  333.5 76.0 %all-gather.3.cloned.1.call-done = bf16[1024,1024]{1,0:T(8,128)(2,1)} async-done(((bf16[32,1024]{1,0:T(8,128)(2,1)}), bf16[1024,1024]{1,0:T(8,128)(2,1)}) %all-gather.3.cloned.1.call-update) | async-done | bytes 2097168 | tf_op jit(solution)/shard_map/all_gather | solution.py:53
  409.5 3.3 fusion.84
  413.0 66.1 %all-reduce.8.cloned.1.call-done = f32[1024,256]{1,0:T(8,128)} async-done(((f32[1024,256]{1,0:T(8,128)}), f32[1024,256]{1,0:T(8,128)}) %all-reduce.8.cloned.1.call-update) | async-done | bytes 1048592 | tf_op jit(solution)/shard_map/psum | solution.py:30
  479.1 1.4 fusion.25
  480.6 0.8 fusion.35
  482.1 2.9 pad_maximum_fusion.3
  485.1 5.9 copy.37
  491.0 5.6 reshape.607
  496.6 5.2 pad_maximum_fusion.1
  501.8 6.8 reshape.609
  509.6 211.0 %reduce-scatter.9.cloned.1.call-done = f32[1,8,5124]{2,1,0:T(8,128)} async-done(((f32[32,8,5124]{2,1,0:T(8,128)}), f32[1,8,5124]{2,1,0:T(8,128)}) %reduce-scatter.9.cloned.1.call-update) | async-done | bytes 163984
  720.6 1.0 reshape.610
  722.1 47.8 %all_gather.10 = bf16[1024,256]{1,0:T(8,128)(2,1)S(1)} all-gather(bf16[32,256]{1,0:T(8,128)(2,1)S(1)} %pad_maximum_fusion.5), channel_id=1, replica_groups=mesh['rows'=32,'tensor'=8] {'rows'}, dimensions={0}, use_global_device_ids=true | all-gather | bytes 540672 | tf_op jit(solution)/shard_map/all_gather | solution.py:180
  771.9 76.5 %all-gather.5.cloned.1.call-done = bf16[1024,1024]{1,0:T(8,128)(2,1)} async-done(((bf16[32,1024]{1,0:T(8,128)(2,1)}), bf16[1024,1024]{1,0:T(8,128)(2,1)}) %all-gather.5.cloned.1.call-update) | async-done | bytes 2097168 | tf_op jit(solution)/shard_map/all_gather | solution.py:53
  848.4 3.4 fusion.85
  851.8 66.3 %all-reduce.10.cloned.1.call-done = f32[1024,256]{1,0:T(8,128)} async-done(((f32[1024,256]{1,0:T(8,128)}), f32[1024,256]{1,0:T(8,128)}) %all-reduce.10.cloned.1.call-update) | async-done | bytes 1048592 | tf_op jit(solution)/shard_map/psum | solution.py:30
  918.1 2.1 fusion.26
  (125 shorter events, 12.4 us)
Async XLA Ops:
  6.5 323.3 %copy-start = (bf16[8,1280,128]{2,1,0:T(8,128)(2,1)S(1)}, bf16[8,1280,128]{2,1,0:T(8,128)(2,1)}, u32[]{:S(2)}) copy-start(bf16[8,1280,128]{2,1,0:T(8,128)(2,1)} %param.20) | copy-start | bytes 7864324
  6.5 78.8 %copy-start.10 = (f32[256]{0:T(256)S(1)}, f32[256]{0:T(256)}, u32[]{:S(2)}) copy-start(f32[256]{0:T(256)} %param.22) | copy-start | bytes 3076
  6.5 78.8 %all-reduce.6.cloned.1.call-start = ((), (), s32[]{:S(2)}) async-start(), calls=%async_computation.2 | async-start | bytes 1048576 | tf_op jit(solution)/shard_map/psum | solution.py:30
  16.2 71.1 %copy-start.6 = (bf16[256,128]{1,0:T(8,128)(2,1)S(1)}, bf16[256,128]{1,0:T(8,128)(2,1)}, u32[]{:S(2)}) copy-start(bf16[256,128]{1,0:T(8,128)(2,1)} %param.25) | copy-start | bytes 196612
  16.2 71.5 %copy-start.7 = (bf16[256,128]{1,0:T(8,128)(2,1)S(1)}, bf16[256,128]{1,0:T(8,128)(2,1)}, u32[]{:S(2)}) copy-start(bf16[256,128]{1,0:T(8,128)(2,1)} %param.24) | copy-start | bytes 196612
  16.2 310.1 %reduce-scatter.7.cloned.1.call-start = ((), (), s32[]{:S(2)}) async-start(), calls=%async_computation.7 | async-start | bytes 5541888
  85.3 2.0 copy-start.2
  114.5 0.7 copy-start.12
  114.5 1.1 copy-start.19
  114.5 295.0 %all-gather.3.cloned.1.call-start = ((), (), s32[]{:S(2)}) async-start(), calls=%async_computation.3 | async-start | bytes 2162688 | tf_op jit(solution)/shard_map/all_gather | solution.py:53
  115.8 0.9 copy-start.16
  115.8 0.9 copy-start.14
  116.4 0.6 copy-start.17
  327.9 3.1 copy-start.22
  327.9 4.2 copy-start.20
  331.9 77.6 %copy-start.21 = (bf16[1024,256]{1,0:T(8,128)(2,1)S(1)}, bf16[1024,256]{1,0:T(8,128)(2,1)}, u32[]{:S(2)}) copy-start(bf16[1024,256]{1,0:T(8,128)(2,1)} %param.26) | copy-start | bytes 1572868
  333.4 147.1 %copy-start.5 = (bf16[256,1024]{1,0:T(8,128)(2,1)S(1)}, bf16[256,1024]{1,0:T(8,128)(2,1)}, u32[]{:S(2)}) copy-start(bf16[256,1024]{1,0:T(8,128)(2,1)} %param.28) | copy-start | bytes 1572868
  333.4 147.1 %copy-start.11 = (f32[256]{0:T(256)S(1)}, f32[256]{0:T(256)}, u32[]{:S(2)}) copy-start(f32[256]{0:T(256)} %param.27) | copy-start | bytes 3076
  333.4 145.7 %all-reduce.8.cloned.1.call-start = ((), (), s32[]{:S(2)}) async-start(), calls=%async_computation.4 | async-start | bytes 2097152 | tf_op jit(solution)/shard_map/psum | solution.py:30
  412.8 307.8 %reduce-scatter.9.cloned.1.call-start = ((), (), s32[]{:S(2)}) async-start(), calls=%async_computation.8 | async-start | bytes 5541888
  480.5 1.3 copy-start.3
  480.6 0.9 copy-start.8
  480.6 1.2 copy-start.9
  508.6 0.7 copy-start.13
  508.6 213.3 %copy-start.15 = (f32[64]{0:T(128)S(1)}, f32[64]{0:T(128)}, u32[]{:S(2)}) copy-start(f32[64]{0:T(128)} %copy-done.14) | copy-start | bytes 772
  508.6 213.3 %copy-start.18 = (f32[32]{0:T(128)S(1)}, f32[32]{0:T(128)}, u32[]{:S(2)}) copy-start(f32[32]{0:T(128)} %copy-done.17) | copy-start | bytes 388
  508.6 339.8 %all-gather.5.cloned.1.call-start = ((), (), s32[]{:S(2)}) async-start(), calls=%async_computation.5 | async-start | bytes 2162688 | tf_op jit(solution)/shard_map/all_gather | solution.py:53
  771.1 146.9 %copy-start.4 = (bf16[1024,256]{1,0:T(8,128)(2,1)S(1)}, bf16[1024,256]{1,0:T(8,128)(2,1)}, u32[]{:S(2)}) copy-start(bf16[1024,256]{1,0:T(8,128)(2,1)} %copy-done.3) | copy-start | bytes 1572868
  771.8 148.4 %copy-start.1 = (bf16[8,1280,128]{2,1,0:T(8,128)(2,1)S(1)}, bf16[8,1280,128]{2,1,0:T(8,128)(2,1)}, u32[]{:S(2)}) copy-start(bf16[8,1280,128]{2,1,0:T(8,128)(2,1)} %param.20) | copy-start | bytes 7864324
  771.8 146.2 %all-reduce.10.cloned.1.call-start = ((), (), s32[]{:S(2)}) async-start(), calls=%async_computation.6 | async-start | bytes 2097152 | tf_op jit(solution)/shard_map/psum | solution.py:30
Sparse Core Ops, SparseCore 0:
  16.3 68.9 all-reduce.5
  114.6 211.6 reduce-scatter.6
  333.5 75.9 all-gather.2
  412.9 66.1 all-reduce.7
  508.7 211.8 reduce-scatter.8
  771.9 76.3 all-gather.4
  851.9 66.1 all-reduce.9
where the time goes:
time: 928 us; the launch traced here: 927 us
  waiting for transfers between devices  774 us (83%)
  local copies, waits for them, and re-layouts  49.3 us (5%)
  blocking collectives  47.8 us (5%)
  other arithmetic  27.3 us (3%)
  between operations  14 us (2%)
  matrix products  13.9 us (1%)
    unnamed x9, waiting for transfers between devices  420 us
    psum x3, waiting for transfers between devices, width_total(): return lax.psum(partial_value, 'tensor')  201 us
    all_gather x2, waiting for transfers between devices, head_mix(): lax.all_gather(attended, 'rows', axis=0, tiled=True)  153 us
    all_gather x1, blocking collectives, per_device(): lax.all_gather(jnp.concatenate([keys_own, values_own], axis=1), 'rows', a...  47.8 us
  transfers between devices with their start and end apart: 7, of which 7 were waited for; matrix products, arithmetic and copies ran while one was open for 0% of the time, Pallas kernels for 0%

commit v1 on v0

--- a/solution.py
+++ b/solution.py
@@ -27,7 +27,7 @@
 
 
 def width_total(partial_value):
-    return lax.psum(partial_value, "tensor")
+    return jnp.sum(lax.all_gather(partial_value, "tensor"), axis=0)
 
 
 def row_scale(summed):

time: 928 us -> 880 us (0.948)
  waiting for transfers between devices: 774 us -> 714 us
  other arithmetic: 27.3 us -> 38.6 us
    psum x3 -> x0, waiting for transfers between devices: 201 us -> none  [width_total(): return lax.psum(partial_value, 'tensor')]
    all_gather x0 -> x3, waiting for transfers between devices: none -> 139 us  [width_total(): return jnp.sum(lax.all_gather(partial_value, 'tensor'), axis=0)]
    reduce_sum x0 -> x3, other arithmetic: none -> 12.5 us  [width_total(): return jnp.sum(lax.all_gather(partial_value, 'tensor'), axis=0)]
where the time goes in v1:
time: 880 us; the launch traced here: 877 us
  waiting for transfers between devices  714 us (81%)
  local copies, waits for them, and re-layouts  49.3 us (6%)
  blocking collectives  47.7 us (5%)
  other arithmetic  38.6 us (4%)
  between operations  14 us (2%)
  matrix products  13.8 us (2%)
    unnamed x9, waiting for transfers between devices  422 us
    all_gather x2, waiting for transfers between devices, head_mix(): lax.all_gather(attended, 'rows', axis=0, tiled=True)  153 us
    all_gather x3, waiting for transfers between devices, width_total(): return jnp.sum(lax.all_gather(partial_value, 'tensor'), axis=0)  139 us
    all_gather x1, blocking collectives, per_device(): lax.all_gather(jnp.concatenate([keys_own, values_own], axis=1), 'rows', a...  47.7 us
  transfers between devices with their start and end apart: 7, of which 7 were waited for; matrix products, arithmetic and copies ran while one was open for 0% of the time, Pallas kernels for 0%

profile of v1, /device:TPU:8, one launch (start us, length us, event | category | flops | bytes accessed | tf_op | source)
XLA Modules:
  0.0 877.4 jit_solution(1633372569032818856)
XLA Ops:
  6.5 0.8 subtract_clamp_fusion
  8.8 6.2 gather_fusion
  15.0 1.1 fusion.31
  16.2 37.6 %all-gather.8.cloned.1.call-done = bf16[8,1024,256]{2,1,0:T(8,128)(2,1)} async-done(((bf16[1,1024,256]{2,1,0:T(8,128)(2,1)}), bf16[8,1024,256]{2,1,0:T(8,128)(2,1)}) %all-gather.8.cloned.1.call-update) | async-done | bytes 4194320 | tf_op jit(solution)/shard_map/all_gather | solution.py:30
  53.8 3.0 reduce_sum.84
  57.1 1.8 fusion.42
  59.6 2.8 pad_maximum_fusion.2
  62.4 5.9 copy.36
  68.3 5.6 reshape.642
  73.9 5.2 pad_maximum_fusion
  79.1 6.8 reshape.644
  88.3 210.3 %reduce-scatter.7.cloned.1.call-done = f32[1,8,5124]{2,1,0:T(8,128)} async-done(((f32[32,8,5124]{2,1,0:T(8,128)}), f32[1,8,5124]{2,1,0:T(8,128)}) %reduce-scatter.7.cloned.1.call-update) | async-done | bytes 163984
  298.6 1.0 reshape.645
  300.2 0.9 broadcast_multiply_fusion.1
  302.1 1.1 fusion.82
  305.7 76.0 %all-gather.10.cloned.1.call-done = bf16[1024,1024]{1,0:T(8,128)(2,1)} async-done(((bf16[32,1024]{1,0:T(8,128)(2,1)}), bf16[1024,1024]{1,0:T(8,128)(2,1)}) %all-gather.10.cloned.1.call-update) | async-done | bytes 2097168 | tf_op jit(solution)/shard_map/all_gather | solution.py:53
  381.8 3.4 fusion.85
  385.4 50.6 %all-gather.14.cloned.1.call-done = f32[8192,256]{1,0:T(8,128)} async-done(((f32[1024,256]{1,0:T(8,128)}), f32[8192,256]{1,0:T(8,128)}) %all-gather.14.cloned.1.call-update) | async-done | bytes 8388624 | tf_op jit(solution)/shard_map/all_gather | solution.py:30
  436.0 4.1 reduce_sum.88
  441.9 2.9 pad_maximum_fusion.3
  444.8 5.9 copy.37
  450.7 5.6 reshape.652
  456.4 5.2 pad_maximum_fusion.1
  461.6 6.8 reshape.654
  469.4 211.8 %reduce-scatter.9.cloned.1.call-done = f32[1,8,5124]{2,1,0:T(8,128)} async-done(((f32[32,8,5124]{2,1,0:T(8,128)}), f32[1,8,5124]{2,1,0:T(8,128)}) %reduce-scatter.9.cloned.1.call-update) | async-done | bytes 163984
  681.3 1.0 reshape.655
  682.7 47.7 %all_gather.29 = bf16[1024,256]{1,0:T(8,128)(2,1)S(1)} all-gather(bf16[32,256]{1,0:T(8,128)(2,1)S(1)} %pad_maximum_fusion.5), channel_id=1, replica_groups=mesh['rows'=32,'tensor'=8] {'rows'}, dimensions={0}, use_global_device_ids=true | all-gather | bytes 540672 | tf_op jit(solution)/shard_map/all_gather | solution.py:180
  732.4 76.5 %all-gather.12.cloned.1.call-done = bf16[1024,1024]{1,0:T(8,128)(2,1)} async-done(((bf16[32,1024]{1,0:T(8,128)(2,1)}), bf16[1024,1024]{1,0:T(8,128)(2,1)}) %all-gather.12.cloned.1.call-update) | async-done | bytes 2097168 | tf_op jit(solution)/shard_map/all_gather | solution.py:53
  808.9 3.4 fusion.86
  812.3 50.8 %all-gather.16.cloned.1.call-done = f32[8192,256]{1,0:T(8,128)} async-done(((f32[1024,256]{1,0:T(8,128)}), f32[8192,256]{1,0:T(8,128)}) %all-gather.16.cloned.1.call-update) | async-done | bytes 8388624 | tf_op jit(solution)/shard_map/all_gather | solution.py:30
  863.1 5.3 reduce_sum.92
  868.4 2.1 fusion.26
  (128 shorter events, 14.2 us)
Async XLA Ops:
  6.5 295.6 %copy-start = (bf16[8,1280,128]{2,1,0:T(8,128)(2,1)S(1)}, bf16[8,1280,128]{2,1,0:T(8,128)(2,1)}, u32[]{:S(2)}) copy-start(bf16[8,1280,128]{2,1,0:T(8,128)(2,1)} %param.20) | copy-start | bytes 7864324
  6.5 47.3 %all-gather.8.cloned.1.call-start = ((), (), s32[]{:S(2)}) async-start(), calls=%async_computation.2 | async-start | bytes 4718592 | tf_op jit(solution)/shard_map/all_gather | solution.py:30
  15.0 42.0 %copy-start.9 = (f32[256]{0:T(256)S(1)}, f32[256]{0:T(256)}, u32[]{:S(2)}) copy-start(f32[256]{0:T(256)} %param.22) | copy-start | bytes 3076
  16.2 282.4 %reduce-scatter.7.cloned.1.call-start = ((), (), s32[]{:S(2)}) async-start(), calls=%async_computation.7 | async-start | bytes 5541888
  57.1 1.9 copy-start.5
  57.1 2.2 copy-start.6
  85.9 0.7 copy-start.11
  85.9 1.1 copy-start.18
  85.9 295.9 %all-gather.10.cloned.1.call-start = ((), (), s32[]{:S(2)}) async-start(), calls=%async_computation.3 | async-start | bytes 2162688 | tf_op jit(solution)/shard_map/all_gather | solution.py:53
  87.1 0.9 copy-start.15
  87.2 0.9 copy-start.13
  87.8 0.6 copy-start.16
  300.2 3.1 copy-start.22
  300.2 4.2 copy-start.19
  304.2 77.6 %copy-start.20 = (bf16[1024,256]{1,0:T(8,128)(2,1)S(1)}, bf16[1024,256]{1,0:T(8,128)(2,1)}, u32[]{:S(2)}) copy-start(bf16[1024,256]{1,0:T(8,128)(2,1)} %param.26) | copy-start | bytes 1572868
  305.7 130.3 %all-gather.14.cloned.1.call-start = ((), (), s32[]{:S(2)}) async-start(), calls=%async_computation.5 | async-start | bytes 9437184 | tf_op jit(solution)/shard_map/all_gather | solution.py:30
  385.2 296.1 %reduce-scatter.9.cloned.1.call-start = ((), (), s32[]{:S(2)}) async-start(), calls=%async_computation.8 | async-start | bytes 5541888
  436.0 4.4 copy-start.4
  436.0 4.4 copy-start.10
  440.3 1.3 copy-start.2
  440.3 0.9 copy-start.7
  440.3 1.2 copy-start.8
  468.3 0.7 copy-start.12
  468.3 214.2 %copy-start.14 = (f32[64]{0:T(128)S(1)}, f32[64]{0:T(128)}, u32[]{:S(2)}) copy-start(f32[64]{0:T(128)} %copy-done.13) | copy-start | bytes 772
  468.3 214.2 %copy-start.17 = (f32[32]{0:T(128)S(1)}, f32[32]{0:T(128)}, u32[]{:S(2)}) copy-start(f32[32]{0:T(128)} %copy-done.16) | copy-start | bytes 388
  468.4 340.6 %all-gather.12.cloned.1.call-start = ((), (), s32[]{:S(2)}) async-start(), calls=%async_computation.4 | async-start | bytes 2162688 | tf_op jit(solution)/shard_map/all_gather | solution.py:53
  730.4 78.5 %copy-start.21 = (bf16[1024,256]{1,0:T(8,128)(2,1)S(1)}, bf16[1024,256]{1,0:T(8,128)(2,1)}, u32[]{:S(2)}) copy-start(bf16[1024,256]{1,0:T(8,128)(2,1)} %param.31) | copy-start | bytes 1572868
  732.4 130.7 %all-gather.16.cloned.1.call-start = ((), (), s32[]{:S(2)}) async-start(), calls=%async_computation.6 | async-start | bytes 9437184 | tf_op jit(solution)/shard_map/all_gather | solution.py:30
  863.1 7.4 copy-start.1
  863.1 5.3 copy-start.3
Sparse Core Ops, SparseCore 0:
  16.3 37.4 all-gather.7
  86.0 212.5 reduce-scatter.6
  305.8 75.9 all-gather.9
  385.3 50.6 all-gather.13
  468.5 212.7 reduce-scatter.8
  732.5 76.3 all-gather.11
  812.4 50.6 all-gather.15
